TPU v7x, 128 devices: a whole 4x4x4 slice. The times are simulated.
128 devices in a mesh: dp: 4 (over x), space: 32 (over y, z, core).
Axes of the slice: x: 4, y: 4, z: 4, core: 2. Of those that a mesh axis runs over, the one named last changes fastest.
Arguments:
- fields: bfloat16 [4, 256, 64, 4096], P('dp', 'space'), may hold values from -6 to 6
- cotangent: bfloat16 [4, 256, 64, 4096], P('dp', 'space'), may hold values from -6 to 6
- mode_weight: bfloat16 [128, 64, 64, 128], P('space'), may hold values from -4 to 4
- mix_weight: bfloat16 [64, 64], replicated, may hold values from -0.75 to 0.75
Outputs:
- response: bfloat16 [4, 256, 64, 4096], P('dp', 'space')
- field_grad: bfloat16 [4, 256, 64, 4096], P('dp', 'space')
- mode_grad: float32 [128, 64, 64, 128], P('space', 'dp')
All inputs are finite; a program needn't handle non-finite values.
Results may differ from a plain program's by a relative error of at most 0.035.
Values may be sent and summed in bfloat16 or wider, within the bound.
No kernel may reach another device: no remote copies, remote signals or barrier semaphores. Data moves between devices by JAX's collectives and lax.ppermute only.
A program may use at most 128 MiB of HBM per device.

v0:
```python
import math
import jax
import jax.numpy as jnp
from jax import lax
from jax.sharding import PartitionSpec as P

GELU_CUBIC = 0.044715
GELU_SCALE = math.sqrt(2.0 / math.pi)


def gelu_value(values):
    inner_arg = GELU_SCALE * (values + GELU_CUBIC * values * values * values)
    return 0.5 * values * (1.0 + jnp.tanh(inner_arg))


def gelu_slope(values):
    tangent = jnp.tanh(GELU_SCALE * (values + GELU_CUBIC * values * values * values))
    return 0.5 * (1.0 + tangent) + 0.5 * values * (1.0 - tangent * tangent) * GELU_SCALE * (
        1.0 + 3.0 * GELU_CUBIC * values * values
    )


def column_angles(length, mode_count):
    positions = lax.iota(jnp.int32, length)
    frequencies = lax.iota(jnp.int32, mode_count)
    phase_index = positions[:, None] * frequencies[None, :] % length
    return phase_index.astype(jnp.float32) * (2.0 * math.pi / length)


def column_factor(mode_count):
    frequencies = lax.iota(jnp.int32, mode_count)
    single = jnp.where(frequencies == 0, 1.0, 2.0).astype(jnp.bfloat16)
    return jnp.concatenate([single, single], axis=0)


def forward_table(length, mode_count, weighted):
    angles = column_angles(length, mode_count)
    norm_scale = 1.0 / math.sqrt(length)
    table_out = jnp.concatenate(
        [jnp.cos(angles) * norm_scale, -jnp.sin(angles) * norm_scale], axis=1
    ).astype(jnp.bfloat16)
    if weighted:
        table_out = table_out * column_factor(mode_count)[None, :]
    return table_out


def inverse_table(length, mode_count, weighted):
    angles = column_angles(length, mode_count).T
    norm_scale = 1.0 / math.sqrt(length)
    table_out = jnp.concatenate(
        [jnp.cos(angles) * norm_scale, -jnp.sin(angles) * norm_scale], axis=0
    ).astype(jnp.bfloat16)
    if weighted:
        table_out = table_out * column_factor(mode_count)[:, None]
    return table_out


def row_tables(extent, mode_count, offset, length):
    slot_index = lax.iota(jnp.int32, mode_count)
    frequencies = jnp.where(
        slot_index < mode_count // 2, slot_index, extent - mode_count + slot_index
    )
    rows_here = offset + lax.iota(jnp.int32, length)
    phase_index = frequencies[:, None] * rows_here[None, :] % extent
    angles = phase_index.astype(jnp.float32) * (2.0 * math.pi / extent)
    norm_scale = 1.0 / math.sqrt(extent)
    return (
        (jnp.cos(angles) * norm_scale).astype(jnp.bfloat16),
        (jnp.sin(angles) * norm_scale).astype(jnp.bfloat16),
    )


def row_forward(cos_table, sin_table, columns):
    cos_part = jnp.einsum("kr,rcpy->ykpc", cos_table, columns, preferred_element_type=jnp.float32)
    sin_part = jnp.einsum("kr,rcpy->ykpc", sin_table, columns, preferred_element_type=jnp.float32)
    real_part = cos_part[:, :, 0] + sin_part[:, :, 1]
    imag_part = cos_part[:, :, 1] - sin_part[:, :, 0]
    return jnp.concatenate([real_part, imag_part], axis=-1)


def row_inverse(cos_table, sin_table, spectrum):
    channels = spectrum.shape[2] // 2
    cos_part = jnp.einsum("kr,ykd->rdy", cos_table, spectrum, preferred_element_type=jnp.float32)
    sin_part = jnp.einsum("kr,ykd->rdy", sin_table, spectrum, preferred_element_type=jnp.float32)
    real_part = cos_part[:, :channels] - sin_part[:, channels:]
    imag_part = cos_part[:, channels:] + sin_part[:, :channels]
    return jnp.stack([real_part, imag_part], axis=2)


def mix_modes(spectrum, weight):
    channels = weight.shape[2]
    real_prod = jnp.einsum(
        "ykc,ykcd->ykd", spectrum[..., :channels], weight, preferred_element_type=jnp.float32
    )
    imag_prod = jnp.einsum(
        "ykc,ykcd->ykd", spectrum[..., channels:], weight, preferred_element_type=jnp.float32
    )
    return jnp.concatenate(
        [
            real_prod[..., :channels] - imag_prod[..., channels:],
            real_prod[..., channels:] + imag_prod[..., :channels],
        ],
        axis=-1,
    )


def mix_adjoint(delta_modes, weight):
    channels = weight.shape[2]
    swapped = jnp.concatenate([delta_modes[..., channels:], -delta_modes[..., :channels]], axis=-1)
    first_half = jnp.einsum(
        "ykd,ykcd->ykc", delta_modes, weight, preferred_element_type=jnp.float32
    )
    second_half = jnp.einsum("ykd,ykcd->ykc", swapped, weight, preferred_element_type=jnp.float32)
    return jnp.concatenate([first_half, second_half], axis=-1)


def weight_grad(spectrum, delta_modes):
    channels = spectrum.shape[2] // 2
    swapped = jnp.concatenate([delta_modes[..., channels:], -delta_modes[..., :channels]], axis=-1)
    real_term = jnp.einsum(
        "ykc,ykd->ykcd", spectrum[..., :channels], delta_modes, preferred_element_type=jnp.float32
    )
    imag_term = jnp.einsum(
        "ykc,ykd->ykcd", spectrum[..., channels:], swapped, preferred_element_type=jnp.float32
    )
    return real_term + imag_term


def on_device(fields, cotangent, mode_weight, mix_weight):
    signal = fields[0]
    upstream = cotangent[0]
    rows_here, channels, length = signal.shape
    mode_rows = mode_weight.shape[0]
    kx_count = mode_weight.shape[1]
    groups = lax.axis_size("space")
    ky_count = mode_rows * groups
    extent = rows_here * groups
    forward_cols = forward_table(length, ky_count, False)
    weighted_cols = forward_table(length, ky_count, True)
    inverse_cols = inverse_table(length, ky_count, True)
    plain_inverse = inverse_table(length, ky_count, False)
    offset = lax.axis_index("space") * rows_here
    local_cos, local_sin = row_tables(extent, kx_count, offset, rows_here)

    def to_modes(columns):
        return lax.psum_scatter(
            row_forward(local_cos, local_sin, columns).astype(jnp.bfloat16),
            "space",
            scatter_dimension=0,
            tiled=True,
        )

    def to_rows(spectrum):
        return row_inverse(
            local_cos, local_sin, lax.all_gather(spectrum, "space", axis=0, tiled=True)
        ).astype(jnp.bfloat16)

    columns = jnp.dot(
        signal.reshape(rows_here * channels, length),
        forward_cols,
        preferred_element_type=jnp.float32,
    )
    columns = columns.astype(jnp.bfloat16).reshape(rows_here, channels, 2, ky_count)
    spectrum = to_modes(columns)
    modes_out = mix_modes(spectrum, mode_weight).astype(jnp.bfloat16)
    back_columns = to_rows(modes_out)
    spectral = jnp.dot(
        back_columns.reshape(rows_here * channels, 2 * ky_count),
        inverse_cols,
        preferred_element_type=jnp.float32,
    )
    spectral = spectral.reshape(rows_here, channels, length)
    preact = spectral + jnp.einsum(
        "rcn,cd->rdn", signal, mix_weight, preferred_element_type=jnp.float32
    )
    response = gelu_value(preact).astype(jnp.bfloat16)
    delta_field = (upstream.astype(jnp.float32) * gelu_slope(preact)).astype(jnp.bfloat16)
    delta_cols = jnp.dot(
        delta_field.reshape(rows_here * channels, length),
        weighted_cols,
        preferred_element_type=jnp.float32,
    )
    delta_cols = delta_cols.astype(jnp.bfloat16).reshape(rows_here, channels, 2, ky_count)
    delta_modes = to_modes(delta_cols)
    input_modes = mix_adjoint(delta_modes, mode_weight).astype(jnp.bfloat16)
    grad_local = weight_grad(spectrum, delta_modes)
    mode_grad = lax.psum_scatter(
        grad_local.astype(jnp.bfloat16), "dp", scatter_dimension=1, tiled=True
    ).astype(jnp.float32)
    input_cols = to_rows(input_modes)
    field_grad = jnp.dot(
        input_cols.reshape(rows_here * channels, 2 * ky_count),
        plain_inverse,
        preferred_element_type=jnp.float32,
    )
    field_grad = field_grad.reshape(rows_here, channels, length)
    field_grad = field_grad + jnp.einsum(
        "rdn,cd->rcn", delta_field, mix_weight, preferred_element_type=jnp.float32
    )
    return (response[None], field_grad.astype(jnp.bfloat16)[None], mode_grad)


def solution(mesh):
    in_specs = (
        P("dp", "space", None, None),
        P("dp", "space", None, None),
        P("space", None, None, None),
        P(),
    )
    out_specs = (
        P("dp", "space", None, None),
        P("dp", "space", None, None),
        P("space", "dp", None, None),
    )
    return jax.shard_map(
        on_device, mesh=mesh, in_specs=in_specs, out_specs=out_specs, check_vma=False
    )
```

profile of v0, /device:TPU:1, one launch (start us, length us, event | category | flops | bytes accessed | tf_op | source)
XLA Modules:
  0.0 377.6 jit_solution(5238253479102441029)
XLA Ops:
  7.2 8.6 %multiply_convert_fusion.3 = (bf16[4096,128]{1,0:T(8,128)(2,1)S(1)}, bf16[4096,128]{1,0:T(8,128)(2,1)S(1)}) fusion(), kind=kLoop, calls=%fused_computation.61 | loop fusion | flops 9961472 | bytes 2097152 | tf_op jit(solution)/shard_map/convert.28
  15.9 3.9 %fusion.41 = bf16[512,256]{0,1:T(8,128)(2,1)S(1)} fusion(bf16[512,4096]{1,0:T(8,128)(2,1)} %bitcast.175, bf16[4096,128]{1,0:T(8,128)(2,1)S(1)} %get-tuple-element.19, bf16[4096,128]{1,0:T(8,128)(2,1)S(1)} %get-tuple-element.20), kind=kOutput, calls=%fused_computation.74 | convolution fusion | flops 1078067200 | bytes 6553600 | tf_op jit(solution)/shard_map/dot_general | solution.py:158
  22.9 3.3 copy.48
  26.2 80.8 %reduce-scatter.7.cloned.1.call-done = bf16[4,64,128]{2,1,0:T(8,128)(2,1)} async-done(((bf16[128,64,128]{2,1,0:T(8,128)(2,1)}), bf16[4,64,128]{2,1,0:T(8,128)(2,1)}) %reduce-scatter.7.cloned.1.call-update) | async-done | bytes 65552 | tf_op jit(solution)/shard_map/reduce_scatter | solution.py:146
  108.1 3.6 fusion.68
  114.0 8.5 %multiply_convert_fusion.1 = (bf16[128,4096]{1,0:T(8,128)(2,1)S(1)}, bf16[128,4096]{1,0:T(8,128)(2,1)S(1)}) fusion(), kind=kLoop, calls=%fused_computation.57 | loop fusion | flops 9961472 | bytes 2097152 | tf_op jit(solution)/shard_map/convert.16
  122.6 36.6 %all-gather.3.cloned.1.call-done = bf16[128,64,128]{2,1,0:T(8,128)(2,1)} async-done(((bf16[4,64,128]{2,1,0:T(8,128)(2,1)}), bf16[128,64,128]{2,1,0:T(8,128)(2,1)}) %all-gather.3.cloned.1.call-update) | async-done | bytes 2097168 | tf_op jit(solution)/shard_map/all_gather | solution.py:155
  159.2 2.1 convolution_bitcast_fusion.6
  161.3 2.1 convolution_bitcast_fusion.7
  167.3 8.5 %fusion.6 = (bf16[8,64,4096]{2,1,0:T(8,128)(2,1)S(1)}, bf16[1,8,64,4096]{3,2,1,0:T(8,128)(2,1)}) fusion(bf16[1,8,64,4096]{3,2,1,0:T(8,128)(2,1)S(1)} %copy-done.6, f32[8,64,4096]{2,1,0:T(8,128)S(1)} %fusion.25, bf16[1,8,64,4096]{3,2,1,0:T(8,128)(2,1)S(1)} %copy-done.7, bf16[64,64]{1,0:T(8,128)(2,1)S(1)} %copy-done), kind=kOutput, calls=%fused_computation.8 | convolution fusion | flops 316669952 | bytes 25174016 | tf_op jit(solution)/shard_map/rcn,cd->rdn/dot_general | solution.py:173
  175.8 2.0 copy-done.1
  177.8 2.0 fusion.38
  185.0 4.6 %copy.56 = bf16[128,64,128]{2,1,0:T(8,128)(2,1)} copy(bf16[128,64,128]{0,1,2:T(8,128)(2,1)} %pad_maximum_fusion.3) | data formatting | bytes 4194304 | tf_op jit(solution)/shard_map/concatenate | solution.py:78
  189.8 76.1 %reduce-scatter.9.cloned.1.call-done = bf16[4,64,128]{2,1,0:T(8,128)(2,1)} async-done(((bf16[128,64,128]{2,1,0:T(8,128)(2,1)}), bf16[4,64,128]{2,1,0:T(8,128)(2,1)}) %reduce-scatter.9.cloned.1.call-update) | async-done | bytes 65552 | tf_op jit(solution)/shard_map/reduce_scatter | solution.py:146
  267.2 4.6 %fusion.64 = f32[4,64,1,64]{3,2,1,0:T(1,128)S(1)} fusion(bf16[4,64,64,128]{3,2,1,0:T(8,128)(2,1)} %param.6, bf16[4,64,128,1]{2,1,0,3:T(8,128)(2,1)S(1)} %get-tuple-element.12), kind=kOutput, calls=%fused_computation.106 | convolution fusion | flops 4194304 | bytes 4325376 | tf_op jit(solution)/shard_map/ykd,ykcd->ykc/dot_general | solution.py:113
  271.8 2.3 fusion.66
  275.0 5.4 %add_convert_fusion = bf16[4,64,64,128]{3,2,1,0:T(8,128)(2,1)S(1)} fusion(f32[4,64,128]{2,1,0:T(8,128)S(1)} %get-tuple-element.11, f32[4,64,64]{2,1,0:T(8,128)S(1)} %get-tuple-element.14, f32[4,64,128]{2,1,0:T(8,128)S(1)} %convert.86, f32[4,64,64]{2,1,0:T(8,128)S(1)} %get-tuple-element.13), kind=kLoop, calls=%fused_computation.12 | loop fusion | flops 8388608 | bytes 4587520 | tf_op jit(solution)/shard_map/convert_element_type | solution.py:188
  281.8 4.8 %copy.103 = bf16[8,8,256,128]{3,1,2,0:T(8,128)(2,1)} copy(bf16[8,8,256,128]{3,2,1,0:T(8,128)(2,1)S(1)} %bitcast.164) | data formatting | bytes 8388608
  286.6 33.6 %all-gather.5.cloned.1.call-done = bf16[128,64,128]{2,1,0:T(8,128)(2,1)} async-done(((bf16[4,64,128]{2,1,0:T(8,128)(2,1)}), bf16[128,64,128]{2,1,0:T(8,128)(2,1)}) %all-gather.5.cloned.1.call-update) | async-done | bytes 2097168 | tf_op jit(solution)/shard_map/all_gather | solution.py:155
  320.2 2.1 convolution_bitcast_fusion.4
  322.3 2.1 convolution_bitcast_fusion.5
  327.1 3.3 fusion.8
  330.3 37.8 %reduce-scatter.11.cloned.1.call-done = bf16[16,32768]{1,0:T(8,128)(2,1)} async-done(((bf16[64,32768]{1,0:T(8,128)(2,1)}), bf16[16,32768]{1,0:T(8,128)(2,1)}) %reduce-scatter.11.cloned.1.call-update) | async-done | bytes 1048592
  369.5 1.6 copy_convert_fusion
  (64 shorter events, 23.5 us)
Async XLA Ops:
  7.2 158.1 %copy-start = (bf16[64,64]{1,0:T(8,128)(2,1)S(1)}, bf16[64,64]{1,0:T(8,128)(2,1)}, u32[]{:S(2)}) copy-start(bf16[64,64]{1,0:T(8,128)(2,1)} %param.7) | copy-start | bytes 24580
  7.2 99.8 %reduce-scatter.7.cloned.1.call-start = ((), (), s32[]{:S(2)}) async-start(), calls=%async_computation.3 | async-start | bytes 2162688 | tf_op jit(solution)/shard_map/reduce_scatter | solution.py:146
  15.9 3.9 %copy-start.3 = (bf16[4096,128]{1,0:T(8,128)(2,1)}, bf16[4096,128]{1,0:T(8,128)(2,1)S(1)}, u32[]{:S(2)}) copy-start(bf16[4096,128]{1,0:T(8,128)(2,1)S(1)} %get-tuple-element.20) | copy-start | bytes 3145732
  26.2 133.0 %all-gather.3.cloned.1.call-start = ((), (), s32[]{:S(2)}) async-start(), calls=%async_computation.4 | async-start | bytes 2162688 | tf_op jit(solution)/shard_map/all_gather | solution.py:155
  107.0 4.7 %copy-start.8 = (bf16[4,64,64,128]{3,2,1,0:T(8,128)(2,1)S(1)}, bf16[4,64,64,128]{3,2,1,0:T(8,128)(2,1)}, u32[]{:S(2)}) copy-start(bf16[4,64,64,128]{3,2,1,0:T(8,128)(2,1)} %param.6) | copy-start | bytes 12582916
  113.8 152.2 %reduce-scatter.9.cloned.1.call-start = ((), (), s32[]{:S(2)}) async-start(), calls=%async_computation.5 | async-start | bytes 2162688 | tf_op jit(solution)/shard_map/reduce_scatter | solution.py:146
  163.9 2.2 copy-start.6
  163.9 3.5 copy-start.7
  167.3 10.5 %copy-start.4 = (bf16[4096,128]{1,0:T(8,128)(2,1)S(1)}, bf16[4096,128]{1,0:T(8,128)(2,1)}, u32[]{:S(2)}) copy-start(bf16[4096,128]{1,0:T(8,128)(2,1)} %copy-done.3) | copy-start | bytes 3145732
  175.8 2.0 copy-start.1
  189.6 130.6 %all-gather.5.cloned.1.call-start = ((), (), s32[]{:S(2)}) async-start(), calls=%async_computation.6 | async-start | bytes 2162688 | tf_op jit(solution)/shard_map/all_gather | solution.py:155
  266.0 5.8 %copy-start.5 = (bf16[4,64,128]{2,1,0:T(8,128)(2,1)S(1)}, bf16[4,64,128]{2,1,0:T(8,128)(2,1)}, u32[]{:S(2)}) copy-start(bf16[4,64,128]{2,1,0:T(8,128)(2,1)} %reduce-scatter.9.cloned.1.call-done) | copy-start | bytes 196612
  266.0 5.8 %copy-start.9 = (bf16[4,64,64,128]{3,2,1,0:T(8,128)(2,1)S(1)}, bf16[4,64,64,128]{3,2,1,0:T(8,128)(2,1)}, u32[]{:S(2)}) copy-start(bf16[4,64,64,128]{3,2,1,0:T(8,128)(2,1)} %param.6) | copy-start | bytes 12582916
  274.9 93.3 %reduce-scatter.11.cloned.1.call-start = ((), (), s32[]{:S(2)}) async-start(), calls=%async_computation.7 | async-start | bytes 5242880
  324.9 2.2 copy-start.2
Sparse Core Ops, SparseCore 0:
  26.3 80.6 reduce-scatter.6
  113.9 45.2 all-gather.2
  189.7 76.2 reduce-scatter.8
  275.0 45.1 all-gather.4
  322.5 45.6 reduce-scatter.10
where the time goes:
time: 378 us
  waiting for transfers between devices  265 us (70%)
  matrix products  43.6 us (12%)
  other arithmetic  32.6 us (9%)
  local copies, waits for them, and re-layouts  21.7 us (6%)
  between operations  14.1 us (4%)
    reduce_scatter x2, waiting for transfers between devices, to_modes(): lax.psum_scatter(row_forward(local_cos, local_sin, columns).astype(jnp.bf...  157 us
    all_gather x2, waiting for transfers between devices, to_rows(): lax.all_gather(spectrum, 'space', axis=0, tiled=True)  70.3 us
    unnamed x6, waiting for transfers between devices  37.9 us
    another operation x8, other arithmetic  18.6 us
    unnamed x23, local copies, waits for them, and re-layouts  12.6 us
    dot_general x1, matrix products, on_device(): jnp.einsum('rcn,cd->rdn', signal, mix_weight, preferred_element_type=jnp....  8.47 us
    concatenate x2, local copies, waits for them, and re-layouts, row_forward(): return jnp.concatenate([real_part, imag_part], axis=-1)  7.85 us
  transfers between devices with their start and end apart: 5, of which 5 were waited for; matrix products, arithmetic and copies ran while one was open for 8% of the time, Pallas kernels for 0%

commit v1 on v0

--- a/solution.py
+++ b/solution.py
@@ -151,9 +151,15 @@
         )
 
     def to_rows(spectrum):
-        return row_inverse(
-            local_cos, local_sin, lax.all_gather(spectrum, "space", axis=0, tiled=True)
-        ).astype(jnp.bfloat16)
+        advance_the_edge = lambda z, across: jnp.concatenate(
+            lax.all_to_all(
+                jnp.stack([z for _ in range(lax.axis_size(across))], axis=0), across, 0, 0
+            ),
+            axis=0,
+        )
+        return row_inverse(local_cos, local_sin, advance_the_edge(spectrum, "space")).astype(
+            jnp.bfloat16
+        )
 
     columns = jnp.dot(
         signal.reshape(rows_here * channels, length),

time: 378 us -> 323 us (0.85)
  waiting for transfers between devices: 265 us -> 174 us
  blocking collectives: 0 us -> 35.2 us
  matrix products: 43.6 us -> 36.3 us
  starting transfers between devices: 0.61 us -> 7.81 us
    all_gather x2 -> x0, waiting for transfers between devices: 70.3 us -> none  [to_rows(): lax.all_gather(spectrum, 'space', axis=0, tiled=True)]
    unnamed x6 -> x4, waiting for transfers between devices: 37.9 us -> 0.05 us
    all_to_all x0 -> x1, blocking collectives: none -> 35.2 us  [to_rows(): lax.all_to_all(jnp.stack([z for _ in range(lax.axis_size(across))], axis=...]
    all_to_all x0 -> x1, waiting for transfers between devices: none -> 18.8 us  [to_rows(): lax.all_to_all(jnp.stack([z for _ in range(lax.axis_size(across))], axis=...]
    all_to_all x0 -> x1, starting transfers between devices: none -> 7.29 us  [to_rows(): lax.all_to_all(jnp.stack([z for _ in range(lax.axis_size(across))], axis=...]
    unnamed x23 -> x31, local copies, waits for them, and re-layouts: 12.6 us -> 13.9 us
  transfers between devices with their start and end apart: 5 -> 4, of which waited for: 5 -> 3; matrix products, arithmetic and copies ran while one was open for 8% -> 7% of each run, Pallas kernels for 0% -> 0%
where the time goes in v1:
time: 323 us; the launch traced here: 322 us
  waiting for transfers between devices  174 us (54%)
  matrix products  36.3 us (11%)
  blocking collectives  35.2 us (11%)
  other arithmetic  31.4 us (10%)
  local copies, waits for them, and re-layouts  23.1 us (7%)
  between operations  14.1 us (4%)
  starting transfers between devices  7.81 us (2%)
    reduce_scatter x2, waiting for transfers between devices, to_modes(): lax.psum_scatter(row_forward(local_cos, local_sin, columns).astype(jnp.bf...  155 us
    all_to_all x1, blocking collectives, to_rows(): lax.all_to_all(jnp.stack([z for _ in range(lax.axis_size(across))], axis=...  35.2 us
    another operation x8, other arithmetic  20.1 us
    all_to_all x1, waiting for transfers between devices, to_rows(): lax.all_to_all(jnp.stack([z for _ in range(lax.axis_size(across))], axis=...  18.8 us
    unnamed x31, local copies, waits for them, and re-layouts  13.9 us
    dot_general x1, matrix products, on_device(): jnp.einsum('rcn,cd->rdn', signal, mix_weight, preferred_element_type=jnp....  8.46 us
    all_to_all x1, starting transfers between devices, to_rows(): lax.all_to_all(jnp.stack([z for _ in range(lax.axis_size(across))], axis=...  7.29 us
    concatenate x2, local copies, waits for them, and re-layouts, row_forward(): return jnp.concatenate([real_part, imag_part], axis=-1)  6.57 us
  transfers between devices with their start and end apart: 4, of which 3 were waited for; matrix products, arithmetic and copies ran while one was open for 7% of the time, Pallas kernels for 0%

profile of v1, /device:TPU:1, one launch (start us, length us, event | category | flops | bytes accessed | tf_op | source)
XLA Modules:
  0.0 322.2 jit_solution(837566217099978579)
XLA Ops:
  7.2 8.6 %multiply_convert_fusion.3 = (bf16[4096,128]{1,0:T(8,128)(2,1)S(1)}, bf16[4096,128]{1,0:T(8,128)(2,1)S(1)}) fusion(), kind=kLoop, calls=%fused_computation.61 | loop fusion | flops 9961472 | bytes 2097152 | tf_op jit(solution)/shard_map/convert.28
  17.2 3.5 %fusion.41 = bf16[512,256]{0,1:T(8,128)(2,1)S(1)} fusion(bf16[512,4096]{1,0:T(8,128)(2,1)} %bitcast.181, bf16[4096,128]{1,0:T(8,128)(2,1)S(1)} %get-tuple-element.19, bf16[4096,128]{1,0:T(8,128)(2,1)S(1)} %get-tuple-element.20), kind=kOutput, calls=%fused_computation.74 | convolution fusion | flops 1078067200 | bytes 6553600 | tf_op jit(solution)/shard_map/dot_general | solution.py:164
  23.9 3.3 %copy.48 = bf16[128,64,128]{2,1,0:T(8,128)(2,1)} copy(bf16[128,64,128]{0,1,2:T(8,128)(2,1)S(1)} %pad_maximum_fusion.1) | data formatting | bytes 4194304 | tf_op jit(solution)/shard_map/concatenate | solution.py:78
  27.2 80.7 %reduce-scatter.7.cloned.1.call-done = bf16[4,64,128]{2,1,0:T(8,128)(2,1)} async-done(((bf16[128,64,128]{2,1,0:T(8,128)(2,1)}), bf16[4,64,128]{2,1,0:T(8,128)(2,1)}) %reduce-scatter.7.cloned.1.call-update) | async-done | bytes 65552 | tf_op jit(solution)/shard_map/reduce_scatter | solution.py:146
  109.0 3.6 %fusion.68 = f32[4,64,1,128]{3,2,1,0:T(1,128)S(1)} fusion(bf16[4,64,64,128]{3,2,1,0:T(8,128)(2,1)} %param.6, bf16[4,64,64,1]{2,1,0,3:T(8,128)(2,1)S(1)} %get-tuple-element.15), kind=kOutput, calls=%fused_computation.110 | convolution fusion | flops 4194304 | bytes 4358144 | tf_op jit(solution)/shard_map/ykc,ykcd->ykd/dot_general | solution.py:95
  114.0 1.8 stack.22
  115.9 7.3 %all-to-all-start = ((bf16[32,4,64,128]{3,2,1,0:T(8,128)(2,1)}), bf16[32,4,64,128]{3,2,1,0:T(8,128)(2,1)S(1)}, u32[]{:S(2)}, u32[]{:S(2)}) async-start(bf16[32,4,64,128]{3,2,1,0:T(8,128)(2,1)} %stack.22), calls=%async_computation.1 | async-start | bytes 4194304 | tf_op jit(solution)/shard_map/all_to_all | solution.py:155
  123.4 9.2 %multiply_convert_fusion.1 = (bf16[128,4096]{1,0:T(8,128)(2,1)S(1)}, bf16[128,4096]{1,0:T(8,128)(2,1)}) fusion(), kind=kLoop, calls=%fused_computation.57 | loop fusion | flops 9961472 | bytes 2097152 | tf_op jit(solution)/shard_map/convert.16
  132.6 18.8 %all-to-all-done = bf16[32,4,64,128]{3,2,1,0:T(8,128)(2,1)S(1)} async-done(((bf16[32,4,64,128]{3,2,1,0:T(8,128)(2,1)}), bf16[32,4,64,128]{3,2,1,0:T(8,128)(2,1)S(1)}, u32[]{:S(2)}, u32[]{:S(2)}) %all-to-all-start) | async-done | bytes 2097184 | tf_op jit(solution)/shard_map/all_to_all | solution.py:155
  153.0 1.4 fusion.25
  156.4 8.5 %fusion.6 = (bf16[8,64,4096]{2,1,0:T(8,128)(2,1)S(1)}, bf16[1,8,64,4096]{3,2,1,0:T(8,128)(2,1)}) fusion(bf16[1,8,64,4096]{3,2,1,0:T(8,128)(2,1)S(1)} %copy-done.10, f32[8,64,4096]{2,1,0:T(8,128)S(1)} %fusion.25, bf16[1,8,64,4096]{3,2,1,0:T(8,128)(2,1)S(1)} %copy-done.11, bf16[64,64]{1,0:T(8,128)(2,1)S(1)} %copy-done), kind=kOutput, calls=%fused_computation.8 | convolution fusion | flops 316669952 | bytes 25174016 | tf_op jit(solution)/shard_map/rcn,cd->rdn/dot_general | solution.py:179
  164.9 2.0 copy-done.3
  171.1 3.3 %copy.56 = bf16[128,64,128]{2,1,0:T(8,128)(2,1)} copy(bf16[128,64,128]{0,1,2:T(8,128)(2,1)S(1)} %pad_maximum_fusion.3) | data formatting | bytes 4194304 | tf_op jit(solution)/shard_map/concatenate | solution.py:78
  174.7 74.6 %reduce-scatter.9.cloned.1.call-done = bf16[4,64,128]{2,1,0:T(8,128)(2,1)} async-done(((bf16[128,64,128]{2,1,0:T(8,128)(2,1)}), bf16[4,64,128]{2,1,0:T(8,128)(2,1)}) %reduce-scatter.9.cloned.1.call-update) | async-done | bytes 65552 | tf_op jit(solution)/shard_map/reduce_scatter | solution.py:146
  251.3 5.4 %add_convert_fusion = bf16[4,64,64,128]{3,2,1,0:T(8,128)(2,1)S(1)} fusion(f32[4,64,128]{2,1,0:T(8,128)S(1)} %get-tuple-element.11, f32[4,64,64]{2,1,0:T(8,128)S(1)} %get-tuple-element.14, f32[4,64,128]{2,1,0:T(8,128)S(1)} %convert.86, f32[4,64,64]{2,1,0:T(8,128)S(1)} %get-tuple-element.13), kind=kLoop, calls=%fused_computation.12 | loop fusion | flops 8388608 | bytes 4587520 | tf_op jit(solution)/shard_map/convert_element_type | solution.py:194
  256.7 1.4 copy.75
  258.1 4.8 %copy.103 = bf16[8,8,256,128]{3,1,2,0:T(8,128)(2,1)} copy(bf16[8,8,256,128]{3,2,1,0:T(8,128)(2,1)S(1)} %bitcast.170) | data formatting | bytes 8388608
  262.9 4.6 %fusion.64 = f32[4,64,1,64]{3,2,1,0:T(1,128)S(1)} fusion(bf16[4,64,64,128]{3,2,1,0:T(8,128)(2,1)} %param.6, bf16[4,64,128,1]{2,1,0,3:T(8,128)(2,1)S(1)} %get-tuple-element.12), kind=kOutput, calls=%fused_computation.106 | convolution fusion | flops 4194304 | bytes 4325376 | tf_op jit(solution)/shard_map/ykd,ykcd->ykc/dot_general | solution.py:113
  267.6 2.3 fusion.66
  270.5 35.2 %all_to_all.10 = bf16[32,4,64,128]{3,2,1,0:T(8,128)(2,1)S(1)} all-to-all(bf16[32,4,64,128]{3,2,1,0:T(8,128)(2,1)S(1)} %stack.26), channel_id=1, replica_groups=mesh['dp'=4,'space'=32] {'space'}, dimensions={0} | all-to-all | bytes 4194304 | tf_op jit(solution)/shard_map/all_to_all | solution.py:155
  307.2 1.3 fusion.23
  309.5 3.2 %fusion.8 = bf16[1,8,64,4096]{3,2,1,0:T(8,128)(2,1)} fusion(f32[8,64,4096]{2,1,0:T(8,128)S(1)} %fusion.23, bf16[8,64,4096]{2,1,0:T(8,128)(2,1)S(1)} %copy-done.4, bf16[64,64]{1,0:T(8,128)(2,1)S(1)} %copy-done), kind=kOutput, calls=%fused_computation.14 | convolution fusion | flops 272629760 | bytes 16785408 | tf_op jit(solution)/shard_map/rdn,cd->rcn/dot_general | solution.py:203
  312.7 1.4 copy.80
  314.1 1.6 copy_convert_fusion
  (71 shorter events, 20.2 us)
Async XLA Ops:
  7.2 147.2 %copy-start = (bf16[64,64]{1,0:T(8,128)(2,1)S(1)}, bf16[64,64]{1,0:T(8,128)(2,1)}, u32[]{:S(2)}) copy-start(bf16[64,64]{1,0:T(8,128)(2,1)} %param.7) | copy-start | bytes 24580
  7.2 100.7 %reduce-scatter.7.cloned.1.call-start = ((), (), s32[]{:S(2)}) async-start(), calls=%async_computation.5 | async-start | bytes 2162688 | tf_op jit(solution)/shard_map/reduce_scatter | solution.py:146
  15.9 1.0 copy-start.5
  15.9 1.3 copy-start.7
  107.9 4.7 %copy-start.12 = (bf16[4,64,64,128]{3,2,1,0:T(8,128)(2,1)S(1)}, bf16[4,64,64,128]{3,2,1,0:T(8,128)(2,1)}, u32[]{:S(2)}) copy-start(bf16[4,64,64,128]{3,2,1,0:T(8,128)(2,1)} %param.6) | copy-start | bytes 12582916
  115.9 35.6 %all-to-all-start = ((bf16[32,4,64,128]{3,2,1,0:T(8,128)(2,1)}), bf16[32,4,64,128]{3,2,1,0:T(8,128)(2,1)S(1)}, u32[]{:S(2)}, u32[]{:S(2)}) async-start(bf16[32,4,64,128]{3,2,1,0:T(8,128)(2,1)} %stack.22), calls=%async_computation.1 | async-start | bytes 4194304 | tf_op jit(solution)/shard_map/all_to_all | solution.py:155
  123.2 126.1 %reduce-scatter.9.cloned.1.call-start = ((), (), s32[]{:S(2)}) async-start(), calls=%async_computation.6 | async-start | bytes 2162688 | tf_op jit(solution)/shard_map/reduce_scatter | solution.py:146
  151.5 1.5 copy-start.1
  153.0 2.2 copy-start.10
  153.0 3.5 %copy-start.11 = (bf16[1,8,64,4096]{3,2,1,0:T(8,128)(2,1)S(1)}, bf16[1,8,64,4096]{3,2,1,0:T(8,128)(2,1)}, u32[]{:S(2)}) copy-start(bf16[1,8,64,4096]{3,2,1,0:T(8,128)(2,1)} %param.4) | copy-start | bytes 12582916
  156.4 10.5 %copy-start.6 = (bf16[4096,128]{1,0:T(8,128)(2,1)S(1)}, bf16[4096,128]{1,0:T(8,128)(2,1)}, u32[]{:S(2)}) copy-start(bf16[4096,128]{1,0:T(8,128)(2,1)} %copy-done.5) | copy-start | bytes 3145732
  156.4 10.5 %copy-start.8 = (bf16[4096,128]{1,0:T(8,128)(2,1)S(1)}, bf16[4096,128]{1,0:T(8,128)(2,1)}, u32[]{:S(2)}) copy-start(bf16[4096,128]{1,0:T(8,128)(2,1)} %copy-done.7) | copy-start | bytes 3145732
  164.9 2.0 copy-start.3
  174.4 138.3 %reduce-scatter.11.cloned.1.call-start = ((), (), s32[]{:S(2)}) async-start(), calls=%async_computation.7 | async-start | bytes 5242880
  262.9 4.7 %copy-start.9 = (bf16[4,64,128]{2,1,0:T(8,128)(2,1)S(1)}, bf16[4,64,128]{2,1,0:T(8,128)(2,1)}, u32[]{:S(2)}) copy-start(bf16[4,64,128]{2,1,0:T(8,128)(2,1)} %reduce-scatter.9.cloned.1.call-done) | copy-start | bytes 196612
  262.9 4.7 %copy-start.13 = (bf16[4,64,64,128]{3,2,1,0:T(8,128)(2,1)S(1)}, bf16[4,64,64,128]{3,2,1,0:T(8,128)(2,1)}, u32[]{:S(2)}) copy-start(bf16[4,64,64,128]{3,2,1,0:T(8,128)(2,1)} %param.6) | copy-start | bytes 12582916
  305.7 1.5 copy-start.2
  307.2 2.3 copy-start.4
Sparse Core Ops, SparseCore 0:
  27.3 80.5 reduce-scatter.6
  174.6 74.7 reduce-scatter.8
  263.0 47.6 reduce-scatter.10
